TPU v7x, 128 devices: a whole 4x4x4 slice. The times are simulated.
128 devices in a mesh: dp: 8 (over z, x_hi), mp: 16 (over y, x_lo, core).
Axes of the slice: x: 4 (x_hi: 2, x_lo: 2; x = x_hi * 2 + x_lo), y: 4, z: 4, core: 2. Of those that a mesh axis runs over, the one named last changes fastest.
Arguments:
- tokens: bfloat16 [16384, 2048], P(('dp', 'mp')), may hold values from -6 to 6
- attn_gain: float32 [2048], replicated, may hold values from 0.25 to 1.75
- mlp_gain: float32 [2048], replicated, may hold values from 0.25 to 1.75
- query_weight: bfloat16 [2048, 2048], replicated, as said below
- keyval_weight: bfloat16 [2048, 1024], replicated, as said below
- output_weight: bfloat16 [2048, 2048], replicated, may hold values from -0.125 to 0.125
- gate_rows: float32 [2048, 8192], P(('dp', 'mp')), may hold values from -0.125 to 0.125
- up_rows: float32 [2048, 8192], P(('dp', 'mp')), may hold values from -0.125 to 0.125
- down_rows: float32 [8192, 2048], P(('dp', 'mp')), may hold values from -0.0625 to 0.0625
- lengths: int32 [8, 1], P('dp'), may hold values from 1024 to 2048
- valid: int32 [16384], P(('dp', 'mp')), may hold values 0 or 1
- page_table: int32 [1024, 1], P(('dp', 'mp')), may hold values from 0 to 7; in each aligned block of 8 rows (0 to 7, 8 to 15, ...) at most 2 rows name the same one
Outputs:
- layer_out: bfloat16 [16384, 2048], P(('dp', 'mp'))
- page_cache: bfloat16 [8, 16, 8, 2, 16, 1024], P('dp', 'mp')
Inputs may be any that keep to these rules, and one draw needn't show every extreme that they name: `page_table`: of the 8 pages of one device at most 2 name the same holder; in every draw some device sends 2 pages to one holder. `query_weight`: entries are independent, of mean zero. `keyval_weight`: entries are independent, of mean zero.
All inputs are finite; a program needn't handle non-finite values. No bound on the sum of `valid` on one device may be relied on, other than what follows from the above.
Results may differ from a plain program's by a relative error of at most 0.02.
The roundings to bfloat16 on the way count: a program that leaves them out, or rounds other values in their place, can miss the bound.
Values may be sent and summed in bfloat16 or wider, within the bound.
A program may use at most 128 MiB of HBM per device.

v0:
```python
import jax
import jax.numpy as jnp
from jax import lax
from jax.sharding import PartitionSpec as P

QH = 32
KVH = 8
HD = 64
PAGE = 16
PAGE_MOST = 2
rope_base = 500000.0


def rms_scale(values, gain):
    mean_square = jnp.mean(values * values, axis=-1, keepdims=True)
    return values * lax.rsqrt(mean_square + 1e-05) * gain


def prompt_ids(lens, rows):
    ends = jnp.cumsum(lens)
    starts = ends - lens
    segment = jnp.sum((rows[:, None] >= ends[None, :]).astype(jnp.int32), axis=1)
    prompt_range = jnp.arange(lens.shape[0], dtype=jnp.int32)
    first = jnp.sum(
        jnp.where(segment[:, None] == prompt_range[None, :], starts[None, :], 0), axis=1
    )
    return (segment, rows - first)


def rotate(heads, position):
    half = heads.shape[-1] // 2
    expo = jnp.arange(half, dtype=jnp.float32) * (2.0 / heads.shape[-1])
    inverse = jnp.exp(-expo * jnp.log(jnp.float32(rope_base)))
    angle = position.astype(jnp.float32)[:, None] * inverse[None, :]
    cosine = jnp.cos(angle)[:, None, :]
    sine = jnp.sin(angle)[:, None, :]
    first_half = heads[..., :half]
    second_half = heads[..., half:]
    return jnp.concatenate(
        [first_half * cosine - second_half * sine, second_half * cosine + first_half * sine],
        axis=-1,
    )


def on_device(
    tokens,
    attn_gain,
    mlp_gain,
    query_weight,
    keyval_weight,
    output_weight,
    gate_rows,
    up_rows,
    down_rows,
    lengths,
    valid,
    page_table,
):
    mp_count = lax.axis_size("mp")
    dp_count = lax.axis_size("dp")
    column = lax.axis_index("mp")
    tok_dev = tokens.shape[0]
    tok_grp = tok_dev * mp_count
    heads_dev = QH // mp_count
    lens = lengths[0]
    local_rows = column * tok_dev + jnp.arange(tok_dev, dtype=jnp.int32)
    unused_segment, position = prompt_ids(lens, local_rows)
    tokens_f = tokens.astype(jnp.float32)
    normed = rms_scale(tokens_f, attn_gain).astype(jnp.bfloat16)
    queries = jnp.dot(normed, query_weight, preferred_element_type=jnp.float32).reshape(
        tok_dev, QH, HD
    )
    queries = rotate(queries, position).astype(jnp.bfloat16)
    keyval = jnp.dot(normed, keyval_weight, preferred_element_type=jnp.float32)
    keys = rotate(keyval[:, : KVH * HD].reshape(tok_dev, KVH, HD), position).astype(jnp.bfloat16)
    values = keyval[:, KVH * HD :].reshape(tok_dev, KVH, HD).astype(jnp.bfloat16)
    query_send = queries.reshape(tok_dev, mp_count, heads_dev * HD)
    pair_send = jnp.repeat(jnp.concatenate([keys, values], axis=-1), mp_count // KVH, axis=1)
    flag_send = jnp.broadcast_to(valid.astype(jnp.bfloat16)[:, None, None], (tok_dev, mp_count, 1))
    query_in, pair_in, flag_in = (
        lax.all_to_all(query_send, "mp", split_axis=1, concat_axis=0, tiled=True),
        lax.all_to_all(pair_send, "mp", split_axis=1, concat_axis=0, tiled=True),
        lax.all_to_all(flag_send, "mp", split_axis=1, concat_axis=0, tiled=True),
    )
    query_in = query_in.reshape(tok_grp, heads_dev, HD)
    key_in = pair_in[:, 0, :HD]
    value_in = pair_in[:, 0, HD:]
    key_open = flag_in[:, 0, 0] > 0.5
    group_rows = jnp.arange(tok_grp, dtype=jnp.int32)
    segment_all, unused_position = prompt_ids(lens, group_rows)
    block_rows = min(512, tok_grp)

    def attend_block(block_index):
        start = block_index * block_rows
        query_block = lax.dynamic_slice_in_dim(query_in, start, block_rows, 0)
        query_rows = start + jnp.arange(block_rows, dtype=jnp.int32)
        query_segment = lax.dynamic_slice_in_dim(segment_all, start, block_rows, 0)
        scores = (
            jnp.einsum("thd,sd->hts", query_block, key_in, preferred_element_type=jnp.float32)
            * 0.125
        )
        allowed = (
            (query_segment[:, None] == segment_all[None, :])
            & (group_rows[None, :] <= query_rows[:, None])
            & (key_open[None, :] | (group_rows[None, :] == query_rows[:, None]))
        )
        scores = jnp.where(allowed[None], scores, jnp.float32(-1e30))
        top = jnp.max(scores, axis=-1, keepdims=True)
        expd = jnp.exp(scores - top)
        weights = (expd / jnp.sum(expd, axis=-1, keepdims=True)).astype(jnp.bfloat16)
        mixed = jnp.einsum("hts,sd->thd", weights, value_in, preferred_element_type=jnp.float32)
        return mixed.astype(jnp.bfloat16).reshape(block_rows, heads_dev * HD)

    attended = lax.map(attend_block, jnp.arange(tok_grp // block_rows, dtype=jnp.int32))
    attended = attended.reshape(tok_grp, heads_dev * HD)
    attended_back = lax.all_to_all(attended, "mp", split_axis=0, concat_axis=1, tiled=True)
    hidden_state = (
        tokens_f + jnp.dot(attended_back, output_weight, preferred_element_type=jnp.float32)
    ).astype(jnp.bfloat16)
    hidden_f = hidden_state.astype(jnp.float32)
    mlp_in = rms_scale(hidden_f, mlp_gain).astype(jnp.bfloat16)
    mlp_group = lax.all_gather(mlp_in, "mp", axis=0, tiled=True)
    rows_dev = gate_rows.shape[0]
    block_width = gate_rows.shape[1] // (dp_count * mp_count)

    def arrange(weight_rows):
        shaped = weight_rows.astype(jnp.bfloat16).reshape(rows_dev, dp_count, mp_count, block_width)
        return jnp.transpose(shaped, (0, 2, 1, 3)).reshape(
            rows_dev, mp_count, dp_count * block_width
        )

    gate_piece, up_piece = (
        lax.all_to_all(arrange(gate_rows), "mp", split_axis=1, concat_axis=0, tiled=True),
        lax.all_to_all(arrange(up_rows), "mp", split_axis=1, concat_axis=0, tiled=True),
    )
    gate_piece = gate_piece.reshape(rows_dev * mp_count, dp_count * block_width)
    up_piece = up_piece.reshape(rows_dev * mp_count, dp_count * block_width)
    gate_block, up_block = (
        lax.all_gather(gate_piece, "dp", axis=0, tiled=True),
        lax.all_gather(up_piece, "dp", axis=0, tiled=True),
    )
    gate = jnp.dot(mlp_group, gate_block, preferred_element_type=jnp.float32)
    upper = jnp.dot(mlp_group, up_block, preferred_element_type=jnp.float32)
    activated = (jax.nn.silu(gate) * upper).astype(jnp.bfloat16)
    down_block = lax.all_gather(down_rows.astype(jnp.bfloat16), "dp", axis=0, tiled=True)
    mlp_sum = lax.psum_scatter(
        jnp.dot(activated, down_block, preferred_element_type=jnp.float32).astype(jnp.bfloat16),
        "mp",
        scatter_dimension=0,
        tiled=True,
    ).astype(jnp.float32)
    layer_out = (hidden_f + mlp_sum).astype(jnp.bfloat16)
    pages_dev = tok_dev // PAGE
    feature = 2 * KVH * HD
    cache_rows = jnp.concatenate(
        [keys.reshape(tok_dev, KVH * HD), values.reshape(tok_dev, KVH * HD)], axis=1
    )
    holders = page_table[:, 0]
    order = jnp.arange(pages_dev, dtype=jnp.int32)
    same_earlier = (holders[None, :] == holders[:, None]) & (order[None, :] < order[:, None])
    rank = jnp.sum(same_earlier.astype(jnp.int32), axis=1)
    target = holders * PAGE_MOST + rank
    slot_range = jnp.arange(dp_count * PAGE_MOST, dtype=jnp.int32)
    placing = (slot_range[:, None] == target[None, :]).astype(jnp.bfloat16)
    flat_pages = cache_rows.reshape(pages_dev, PAGE * feature)
    page_send = jnp.dot(placing, flat_pages, preferred_element_type=jnp.float32).astype(
        jnp.bfloat16
    )
    page_send = page_send.reshape(dp_count, PAGE_MOST, PAGE, feature)
    received = lax.all_to_all(page_send, "dp", split_axis=0, concat_axis=0, tiled=True)
    page_cache = received[None, None]
    return (layer_out, page_cache)


def solution(mesh):
    return jax.shard_map(
        on_device,
        mesh=mesh,
        in_specs=(
            P(("dp", "mp"), None),
            P(),
            P(),
            P(),
            P(),
            P(),
            P(("dp", "mp"), None),
            P(("dp", "mp"), None),
            P(("dp", "mp"), None),
            P("dp", None),
            P(("dp", "mp")),
            P(("dp", "mp"), None),
        ),
        out_specs=(P(("dp", "mp"), None), P("dp", "mp", None, None, None, None)),
        check_vma=False,
    )
```

profile of v0, /device:TPU:4, one launch (start us, length us, event | category | flops | bytes accessed | tf_op | source)
XLA Modules:
  0.0 442.2 jit_solution(11806712546734390694)
XLA Ops:
  7.2 0.7 convert_element_type.100
  7.9 0.6 broadcast_in_dim.28
  8.5 5.2 %all-to-all-start = ((bf16[128,16,1]{0,2,1:T(2,128)(2,1)}), bf16[128,16,1]{0,2,1:T(2,128)(2,1)S(1)}, u32[]{:S(2)}, u32[]{:S(2)}) async-start(bf16[128,16,1]{0,2,1:T(2,128)(2,1)} %broadcast_in_dim.28), calls=%async_computation | async-start | bytes 16384 | tf_op jit(solution)/shard_map/all_to_all | solution.py:83
  13.7 1.2 fusion.37
  15.0 3.1 fusion.40
  19.5 0.9 copy.77
  20.4 5.7 %all-to-all-start.4 = ((bf16[16,16,512]{2,0,1:T(8,128)(2,1)}), bf16[16,16,512]{2,0,1:T(8,128)(2,1)S(1)}, u32[]{:S(2)}, u32[]{:S(2)}) async-start(bf16[16,16,512]{2,0,1:T(8,128)(2,1)} %copy.77), calls=%async_computation.4 | async-start | bytes 524288 | tf_op jit(solution)/shard_map/all_to_all | solution.py:133
  26.3 7.8 %all-to-all-done.4 = bf16[16,16,512]{2,0,1:T(8,128)(2,1)S(1)} async-done(((bf16[16,16,512]{2,0,1:T(8,128)(2,1)}), bf16[16,16,512]{2,0,1:T(8,128)(2,1)S(1)}, u32[]{:S(2)}, u32[]{:S(2)}) %all-to-all-start.4) | async-done | bytes 262176 | tf_op jit(solution)/shard_map/all_to_all | solution.py:133
  34.1 0.9 broadcast_in_dim.29
  35.0 3.6 all-to-all-start.2
  38.6 6.8 %fusion.42 = f32[128,2048]{0,1:T(8,128)S(1)} fusion(bf16[2048,2048]{1,0:T(8,128)(2,1)} %param.17, bf16[128,2048]{1,0:T(8,128)(2,1)S(1)} %copy-done, f32[2048]{0:T(1024)S(1)} %copy-done.6, f32[128]{0:T(128)S(1)} %add_rsqrt_fusion.1), kind=kOutput, calls=%fused_computation.57 | convolution fusion | flops 1074790400 | bytes 9970176 | tf_op jit(solution)/shard_map/dot_general | solution.py:70
  46.3 0.9 pad_maximum_fusion
  47.1 2.3 all-to-all-done.2
  49.4 3.6 all-to-all-start.1
  53.1 0.7 all-gather.7.cloned.1.call-update
  54.5 0.9 copy.72
  55.6 8.3 %all-to-all-done.1 = bf16[128,16,128]{0,2,1:T(8,128)(2,1)S(1)} async-done(((bf16[128,16,128]{0,2,1:T(8,128)(2,1)}), bf16[128,16,128]{0,2,1:T(8,128)(2,1)S(1)}, u32[]{:S(2)}, u32[]{:S(2)}) %all-to-all-start.1) | async-done | bytes 524320 | tf_op jit(solution)/shard_map/all_to_all | solution.py:81
  64.5 68.7 %while.12 = (s32[]{:T(128)}, bf16[4,512,128]{2,1,0:T(8,128)(2,1)S(1)}, s32[4]{0:T(128)S(1)}, s32[2048]{0:T(1024)S(1)}, pred[2048]{0:T(1024)(128)(4,1)S(1)}, /*in...) while((s32[]{:T(128)}, ...), condition=%wide.region_4.5_spmd.clone.clone, body=%wide.region_1.0_spmd.clone.clone.sunk | while | flops 555813376 | bytes 20213952 | solution.py:114
  64.5 0.6 dynamic_slice.30
  65.8 3.6 fusion.77
  69.4 7.2 %fusion.78 = (f32[2,512]{1,0:T(2,128)S(1)}, f32[2,512,2048]{2,1,0:T(8,128)}) fusion(pred[512,2048]{1,0:T(8,128)(4,1)S(1)} %fusion.77, bf16[2048,64]{0,1:T(8,128)(2,1)} %get-tuple-element.220, bf16[2048,2,64]{0,2,1:T(8,128)(2,1)S(1)} %get-tuple-element.219, s32[]{:T(128)S(6)} %select_n.41), kind=kOutput, calls=%fused_computation.76.clone.1 | convolution fusion | flops 276826112 | bytes 9834500 | tf_op jit(solution)/shard_map/while/body/eval_jaxpr/sub | solution.py:109
  76.6 4.9 %fusion.79 = bf16[2,512,64]{1,2,0:T(8,128)(2,1)S(1)} fusion(f32[2,512,2048]{2,1,0:T(8,128)} %get-tuple-element.188, f32[2,512]{1,0:T(2,128)S(1)} %get-tuple-element.189, bf16[2048,64]{0,1:T(8,128)(2,1)S(1)} %get-tuple-element.221), kind=kOutput, calls=%fused_computation.17.clone.1 | convolution fusion | flops 272695296 | bytes 8785920 | tf_op jit(solution)/shard_map/while/body/eval_jaxpr/hts,sd->thd/dot_general | solution.py:111
  81.7 0.6 dynamic_slice.30
  83.0 3.6 fusion.77
  86.6 7.2 %fusion.78 = (f32[2,512]{1,0:T(2,128)S(1)}, f32[2,512,2048]{2,1,0:T(8,128)}) fusion(pred[512,2048]{1,0:T(8,128)(4,1)S(1)} %fusion.77, bf16[2048,64]{0,1:T(8,128)(2,1)} %get-tuple-element.220, bf16[2048,2,64]{0,2,1:T(8,128)(2,1)S(1)} %get-tuple-element.219, s32[]{:T(128)S(6)} %select_n.41), kind=kOutput, calls=%fused_computation.76.clone.1 | convolution fusion | flops 276826112 | bytes 9834500 | tf_op jit(solution)/shard_map/while/body/eval_jaxpr/sub | solution.py:109
  93.8 4.9 %fusion.79 = bf16[2,512,64]{1,2,0:T(8,128)(2,1)S(1)} fusion(f32[2,512,2048]{2,1,0:T(8,128)} %get-tuple-element.188, f32[2,512]{1,0:T(2,128)S(1)} %get-tuple-element.189, bf16[2048,64]{0,1:T(8,128)(2,1)S(1)} %get-tuple-element.221), kind=kOutput, calls=%fused_computation.17.clone.1 | convolution fusion | flops 272695296 | bytes 8785920 | tf_op jit(solution)/shard_map/while/body/eval_jaxpr/hts,sd->thd/dot_general | solution.py:111
  98.8 0.6 dynamic_slice.30
  100.2 3.6 fusion.77
  103.8 7.2 %fusion.78 = (f32[2,512]{1,0:T(2,128)S(1)}, f32[2,512,2048]{2,1,0:T(8,128)}) fusion(pred[512,2048]{1,0:T(8,128)(4,1)S(1)} %fusion.77, bf16[2048,64]{0,1:T(8,128)(2,1)} %get-tuple-element.220, bf16[2048,2,64]{0,2,1:T(8,128)(2,1)S(1)} %get-tuple-element.219, s32[]{:T(128)S(6)} %select_n.41), kind=kOutput, calls=%fused_computation.76.clone.1 | convolution fusion | flops 276826112 | bytes 9834500 | tf_op jit(solution)/shard_map/while/body/eval_jaxpr/sub | solution.py:109
  111.0 4.8 %fusion.79 = bf16[2,512,64]{1,2,0:T(8,128)(2,1)S(1)} fusion(f32[2,512,2048]{2,1,0:T(8,128)} %get-tuple-element.188, f32[2,512]{1,0:T(2,128)S(1)} %get-tuple-element.189, bf16[2048,64]{0,1:T(8,128)(2,1)S(1)} %get-tuple-element.221), kind=kOutput, calls=%fused_computation.17.clone.1 | convolution fusion | flops 272695296 | bytes 8785920 | tf_op jit(solution)/shard_map/while/body/eval_jaxpr/hts,sd->thd/dot_general | solution.py:111
  116.0 0.6 dynamic_slice.30
  117.3 3.6 fusion.77
  121.0 7.2 %fusion.78 = (f32[2,512]{1,0:T(2,128)S(1)}, f32[2,512,2048]{2,1,0:T(8,128)}) fusion(pred[512,2048]{1,0:T(8,128)(4,1)S(1)} %fusion.77, bf16[2048,64]{0,1:T(8,128)(2,1)} %get-tuple-element.220, bf16[2048,2,64]{0,2,1:T(8,128)(2,1)S(1)} %get-tuple-element.219, s32[]{:T(128)S(6)} %select_n.41), kind=kOutput, calls=%fused_computation.76.clone.1 | convolution fusion | flops 276826112 | bytes 9834500 | tf_op jit(solution)/shard_map/while/body/eval_jaxpr/sub | solution.py:109
  128.1 4.8 %fusion.79 = bf16[2,512,64]{1,2,0:T(8,128)(2,1)S(1)} fusion(f32[2,512,2048]{2,1,0:T(8,128)} %get-tuple-element.188, f32[2,512]{1,0:T(2,128)S(1)} %get-tuple-element.189, bf16[2048,64]{0,1:T(8,128)(2,1)S(1)} %get-tuple-element.221), kind=kOutput, calls=%fused_computation.17.clone.1 | convolution fusion | flops 272695296 | bytes 8785920 | tf_op jit(solution)/shard_map/while/body/eval_jaxpr/hts,sd->thd/dot_general | solution.py:111
  133.1 13.5 %all_to_all.96 = bf16[16,128,128]{2,1,0:T(8,128)(2,1)S(1)} all-to-all(bf16[16,128,128]{2,1,0:T(8,128)(2,1)S(1)} %bitcast.125), channel_id=1, replica_groups=mesh['dp'=8,'mp'=16] {'mp'}, dimensions={0} | all-to-all | bytes 1048576 | tf_op jit(solution)/shard_map/all_to_all | solution.py:116
  147.0 4.8 %multiply_reduce_fusion = (f32[128]{0:T(128)S(1)}, f32[128,2048]{1,0:T(8,128)S(1)}) fusion(bf16[128,2048]{0,1:T(8,128)(2,1)S(1)} %bitcast.112, bf16[2048,2048]{1,0:T(8,128)(2,1)} %param.19, bf16[128,2048]{1,0:T(8,128)(2,1)S(1)} %copy-done), kind=kOutput, calls=%fused_computation.44 | convolution fusion | flops 1075314560 | bytes 10486272 | tf_op jit(solution)/shard_map/dot_general | solution.py:118
  151.8 1.0 multiply_convert_fusion.1
  152.8 0.7 convert_element_type.113
  154.9 11.8 %all_to_all.97 = bf16[16,16,512]{2,0,1:T(8,128)(2,1)} all-to-all(bf16[16,16,512]{2,0,1:T(8,128)(2,1)S(1)} %copy.79), channel_id=1, replica_groups=mesh['dp'=8,'mp'=16] {'mp'}, dimensions={1} | all-to-all | bytes 524288 | tf_op jit(solution)/shard_map/all_to_all | solution.py:134
  167.0 38.3 %all-gather.5.cloned.1.call-done = bf16[2048,2048]{1,0:T(8,128)(2,1)} async-done(((bf16[128,2048]{1,0:T(8,128)(2,1)}), bf16[2048,2048]{1,0:T(8,128)(2,1)}) %all-gather.5.cloned.1.call-update) | async-done | bytes 8388624 | tf_op jit(solution)/shard_map/all_gather | solution.py:122
  205.3 10.4 %fusion.57 = f32[2048,512]{1,0:T(8,128)} fusion(bf16[2048,2048]{1,0:T(8,128)(2,1)} %all-gather.5.cloned.1.call-done, bf16[2048,512]{1,0:T(8,128)(2,1)} %all-gather.7.cloned.1.call-done), kind=kOutput, calls=%fused_computation.77 | convolution fusion | flops 4294967296 | bytes 14680064 | tf_op jit(solution)/shard_map/dot_general | solution.py:142
  215.7 45.8 %all-gather.11.cloned.1.call-done = bf16[512,2048]{1,0:T(8,128)(2,1)} async-done(((bf16[64,2048]{1,0:T(8,128)(2,1)}), bf16[512,2048]{1,0:T(8,128)(2,1)}) %all-gather.11.cloned.1.call-update) | async-done | bytes 2097168 | tf_op jit(solution)/shard_map/all_gather | solution.py:145
  261.5 54.1 %all-gather.9.cloned.1.call-done = bf16[2048,512]{1,0:T(8,128)(2,1)} async-done(((bf16[256,512]{1,0:T(8,128)(2,1)}), bf16[2048,512]{1,0:T(8,128)(2,1)}) %all-gather.9.cloned.1.call-update) | async-done | bytes 2097168 | tf_op jit(solution)/shard_map/all_gather | solution.py:140
  315.6 15.2 %convolution_convert_fusion.1 = bf16[2048,2048]{1,0:T(8,128)(2,1)} fusion(bf16[512,2048]{1,0:T(8,128)(2,1)} %all-gather.11.cloned.1.call-done, f32[2048,512]{1,0:T(8,128)} %fusion.57, bf16[2048,2048]{1,0:T(8,128)(2,1)} %all-gather.5.cloned.1.call-done, bf16[2048,512]{1,0:T(8,128)(2,1)} %all-gather.9.cloned.1.call-done), kind=kOutput, calls=%fused_computation.32 | convolution fusion | flops 8600420352 | bytes 25165824 | tf_op jit(solution)/shard_map/dot_general | solution.py:147
  332.3 18.0 %all_to_all.98 = bf16[8,2,16,1024]{3,2,1,0:T(8,128)(2,1)S(1)} all-to-all(bf16[8,2,16,1024]{3,2,1,0:T(8,128)(2,1)S(1)} %bitcast.120), channel_id=1, replica_groups=mesh['dp'=8,'mp'=16] {'dp'}, dimensions={0} | all-to-all | bytes 1048576 | tf_op jit(solution)/shard_map/all_to_all | solution.py:170
  350.3 82.7 %reduce-scatter.2.cloned.1.call-done = bf16[128,2048]{1,0:T(8,128)(2,1)} async-done(((bf16[2048,2048]{1,0:T(8,128)(2,1)}), bf16[128,2048]{1,0:T(8,128)(2,1)}) %reduce-scatter.2.cloned.1.call-update) | async-done | bytes 524304 | tf_op jit(solution)/shard_map/reduce_scatter | solution.py:146
  433.0 1.9 add_convert_fusion
  434.9 0.8 copy.101
  (84 shorter events, 7.4 us)
Async XLA Ops:
  7.2 11.3 %copy-start.2 = (f32[16,8192]{1,0:T(8,128)S(1)}, f32[16,8192]{1,0:T(8,128)}, u32[]{:S(2)}) copy-start(f32[16,8192]{1,0:T(8,128)} %param.20) | copy-start | bytes 1572868
  8.5 11.9 %all-to-all-start = ((bf16[128,16,1]{0,2,1:T(2,128)(2,1)}), bf16[128,16,1]{0,2,1:T(2,128)(2,1)S(1)}, u32[]{:S(2)}, u32[]{:S(2)}) async-start(bf16[128,16,1]{0,2,1:T(2,128)(2,1)} %broadcast_in_dim.28), calls=%async_computation | async-start | bytes 16384 | tf_op jit(solution)/shard_map/all_to_all | solution.py:83
  18.3 20.3 %copy-start = (bf16[128,2048]{1,0:T(8,128)(2,1)S(1)}, bf16[128,2048]{1,0:T(8,128)(2,1)}, u32[]{:S(2)}) copy-start(bf16[128,2048]{1,0:T(8,128)(2,1)} %param.14) | copy-start | bytes 1572868
  18.3 20.3 %copy-start.6 = (f32[2048]{0:T(1024)S(1)}, f32[2048]{0:T(1024)}, u32[]{:S(2)}) copy-start(f32[2048]{0:T(1024)} %param.15) | copy-start | bytes 24580
  20.4 13.8 %all-to-all-start.4 = ((bf16[16,16,512]{2,0,1:T(8,128)(2,1)}), bf16[16,16,512]{2,0,1:T(8,128)(2,1)S(1)}, u32[]{:S(2)}, u32[]{:S(2)}) async-start(bf16[16,16,512]{2,0,1:T(8,128)(2,1)} %copy.77), calls=%async_computation.4 | async-start | bytes 524288 | tf_op jit(solution)/shard_map/all_to_all | solution.py:133
  34.1 11.3 %copy-start.1 = (bf16[16,16,512]{2,0,1:T(8,128)(2,1)}, bf16[16,16,512]{2,0,1:T(8,128)(2,1)S(1)}, u32[]{:S(2)}) copy-start(bf16[16,16,512]{2,0,1:T(8,128)(2,1)S(1)} %all-to-all-done.4) | copy-start | bytes 786436
  35.0 14.4 %all-to-all-start.2 = ((bf16[128,16,128]{0,2,1:T(8,128)(2,1)}), bf16[128,16,128]{0,2,1:T(8,128)(2,1)S(1)}, u32[]{:S(2)}, u32[]{:S(2)}) async-start(bf16[128,16,128]{0,2,1:T(8,128)(2,1)} %bitcast.10), calls=%async_computation.2 | async-start | bytes 1048576 | tf_op jit(solution)/shard_map/all_to_all | solution.py:82
  47.1 17.3 %copy-start.5 = (bf16[4,512,128]{2,1,0:T(8,128)(2,1)S(1)}, bf16[4,512,128]{2,1,0:T(8,128)(2,1)}, u32[]{:S(2)}) copy-start(bf16[4,512,128]{2,1,0:T(8,128)(2,1)} %custom-call) | copy-start | bytes 1572868
  49.4 14.4 %all-to-all-start.1 = ((bf16[128,16,128]{0,2,1:T(8,128)(2,1)}), bf16[128,16,128]{0,2,1:T(8,128)(2,1)S(1)}, u32[]{:S(2)}, u32[]{:S(2)}) async-start(bf16[128,16,128]{0,2,1:T(8,128)(2,1)} %bitcast.5), calls=%async_computation.1 | async-start | bytes 1048576 | tf_op jit(solution)/shard_map/all_to_all | solution.py:81
  53.0 114.0 %all-gather.7.cloned.1.call-start = ((), (), s32[]{:S(2)}) async-start(), calls=%async_computation.9 | async-start | bytes 2359296 | tf_op jit(solution)/shard_map/all_gather | solution.py:139
  53.8 151.5 %all-gather.5.cloned.1.call-start = ((), (), s32[]{:S(2)}) async-start(), calls=%async_computation.8 | async-start | bytes 8912896 | tf_op jit(solution)/shard_map/all_gather | solution.py:122
  146.9 4.9 %copy-start.7 = (f32[2048]{0:T(1024)S(1)}, f32[2048]{0:T(1024)}, u32[]{:S(2)}) copy-start(f32[2048]{0:T(1024)} %param.16) | copy-start | bytes 24580
  146.9 5.9 %copy-start.3 = (f32[64,2048]{1,0:T(8,128)S(1)}, f32[64,2048]{1,0:T(8,128)}, u32[]{:S(2)}) copy-start(f32[64,2048]{1,0:T(8,128)} %param.22) | copy-start | bytes 1572868
  146.9 6.7 %copy-start.4 = (f32[16,8192]{1,0:T(8,128)S(1)}, f32[16,8192]{1,0:T(8,128)}, u32[]{:S(2)}) copy-start(f32[16,8192]{1,0:T(8,128)} %param.21) | copy-start | bytes 1572868
  152.8 108.7 %all-gather.11.cloned.1.call-start = ((), (), s32[]{:S(2)}) async-start(), calls=%async_computation.11 | async-start | bytes 2359296 | tf_op jit(solution)/shard_map/all_gather | solution.py:145
  153.6 162.0 %all-gather.9.cloned.1.call-start = ((), (), s32[]{:S(2)}) async-start(), calls=%async_computation.10 | async-start | bytes 2359296 | tf_op jit(solution)/shard_map/all_gather | solution.py:140
  166.7 266.3 %reduce-scatter.2.cloned.1.call-start = ((), (), s32[]{:S(2)}) async-start(), calls=%async_computation.12 | async-start | bytes 8912896 | tf_op jit(solution)/shard_map/reduce_scatter | solution.py:146
  330.9 0.7 copy-start.8
Sparse Core Ops, SparseCore 0:
  56.2 54.2 all-gather.6
  152.9 52.3 all-gather.4
  208.2 53.2 all-gather.10
  263.7 51.8 all-gather.8
  331.0 101.9 reduce-scatter.1
where the time goes:
time: 443 us; the launch traced here: 442 us
  waiting for transfers between devices  240 us (54%)
  matrix products  88.8 us (20%)
  blocking collectives  43.3 us (10%)
  other arithmetic  21.6 us (5%)
  starting transfers between devices  18.7 us (4%)
  between operations  14.8 us (3%)
  local copies, waits for them, and re-layouts  12.2 us (3%)
    reduce_scatter x1, waiting for transfers between devices, on_device(): lax.psum_scatter(jnp.dot(activated, down_block, preferred_element_type=jn...  82.7 us
    all_gather x1, waiting for transfers between devices, on_device(): lax.all_gather(up_piece, 'dp', axis=0, tiled=True)  54.1 us
    all_gather x1, waiting for transfers between devices, on_device(): lax.all_gather(down_rows.astype(jnp.bfloat16), 'dp', axis=0, tiled=True)  45.8 us
    all_gather x1, waiting for transfers between devices, on_device(): mlp_group = lax.all_gather(mlp_in, 'mp', axis=0, tiled=True)  38.3 us
    sub x4, matrix products, attend_block(): expd = jnp.exp(scores - top)  28.7 us
    dot_general x4, matrix products, attend_block(): jnp.einsum('hts,sd->thd', weights, value_in, preferred_element_type=jnp.f...  19.4 us
    all_to_all x1, blocking collectives, on_device(): lax.all_to_all(page_send, 'dp', split_axis=0, concat_axis=0, tiled=True)  18 us
    dot_general x1, matrix products, on_device(): jnp.dot(activated, down_block, preferred_element_type=jnp.float32)  15.2 us
  transfers between devices with their start and end apart: 9, of which 7 were waited for; matrix products, arithmetic and copies ran while one was open for 23% of the time, Pallas kernels for 0%

commit v1 on v0

--- a/solution.py
+++ b/solution.py
@@ -1,3 +1,4 @@
+import functools
 import jax
 import jax.numpy as jnp
 from jax import lax
@@ -9,6 +10,21 @@
 PAGE = 16
 PAGE_MOST = 2
 rope_base = 500000.0
+
+
+def do_point(local_values, axis_key, row_dim):
+    return jnp.concatenate(
+        jax.lax.all_to_all(
+            jnp.stack([local_values for _ in range(jax.lax.axis_size(axis_key))]),
+            concat_axis=0,
+            split_axis=0,
+            axis_name=axis_key,
+        ),
+        row_dim,
+    )
+
+
+spread_rails = functools.partial(do_point, axis_key="mp", row_dim=0)
 
 
 def rms_scale(values, gain):
@@ -119,7 +135,7 @@
     ).astype(jnp.bfloat16)
     hidden_f = hidden_state.astype(jnp.float32)
     mlp_in = rms_scale(hidden_f, mlp_gain).astype(jnp.bfloat16)
-    mlp_group = lax.all_gather(mlp_in, "mp", axis=0, tiled=True)
+    mlp_group = spread_rails(mlp_in)
     rows_dev = gate_rows.shape[0]
     block_width = gate_rows.shape[1] // (dp_count * mp_count)
 

time: 443 us -> 429 us (0.968)
  blocking collectives: 43.3 us -> 18 us
  starting transfers between devices: 18.7 us -> 30.6 us
  waiting for transfers between devices: 240 us -> 232 us
  local copies, waits for them, and re-layouts: 12.2 us -> 19.7 us
    all_to_all x0 -> x3, waiting for transfers between devices: none -> 122 us  [the longest x1 110 us: do_point(): jax.lax.all_to_all(jnp.stack([local_values for _ in range(jax.lax.axis_si...]
    all_gather x1, waiting for transfers between devices: 54.1 us -> 7.43 us  [on_device(): lax.all_gather(up_piece, 'dp', axis=0, tiled=True)]
    all_gather x1, waiting for transfers between devices: 45.8 us -> 0.01 us  [on_device(): lax.all_gather(down_rows.astype(jnp.bfloat16), 'dp', axis=0, tiled=True)]
    all_gather x1 -> x0, waiting for transfers between devices: 38.3 us -> none  [on_device(): mlp_group = lax.all_gather(mlp_in, 'mp', axis=0, tiled=True)]
    all_to_all x2 -> x0, blocking collectives: 25.3 us -> none  [the longest x1 13.5 us: on_device(): lax.all_to_all(attended, 'mp', split_axis=0, concat_axis=1, tiled=True)]
    all_to_all x0 -> x3, starting transfers between devices: none -> 12 us  [the longest x1 4.89 us: do_point(): jax.lax.all_to_all(jnp.stack([local_values for _ in range(jax.lax.axis_si...]
  transfers between devices with their start and end apart: 9 -> 11, of which waited for: 7 -> 8; matrix products, arithmetic and copies ran while one was open for 23% -> 25% of each run, Pallas kernels for 0% -> 0%
where the time goes in v1:
time: 429 us; the launch traced here: 427 us
  waiting for transfers between devices  232 us (54%)
  matrix products  88.8 us (21%)
  starting transfers between devices  30.6 us (7%)
  other arithmetic  20.8 us (5%)
  local copies, waits for them, and re-layouts  19.7 us (5%)
  blocking collectives  18 us (4%)
  between operations  14.8 us (3%)
    all_to_all x1, waiting for transfers between devices, do_point(): jax.lax.all_to_all(jnp.stack([local_values for _ in range(jax.lax.axis_si...  110 us
    reduce_scatter x1, waiting for transfers between devices, on_device(): lax.psum_scatter(jnp.dot(activated, down_block, preferred_element_type=jn...  82.4 us
    sub x4, matrix products, attend_block(): expd = jnp.exp(scores - top)  28.7 us
    dot_general x4, matrix products, attend_block(): jnp.einsum('hts,sd->thd', weights, value_in, preferred_element_type=jnp.f...  19.4 us
    all_to_all x1, blocking collectives, on_device(): lax.all_to_all(page_send, 'dp', split_axis=0, concat_axis=0, tiled=True)  18 us
    dot_general x1, matrix products, on_device(): jnp.dot(activated, down_block, preferred_element_type=jnp.float32)  15.2 us
    and x4, other arithmetic, attend_block(): (query_segment[:, None] == segment_all[None, :]) & (group_rows[None, :] <...  14.5 us
    dot_general x1, matrix products, on_device(): gate = jnp.dot(mlp_group, gate_block, preferred_element_type=jnp.float32)  10.5 us
  transfers between devices with their start and end apart: 11, of which 8 were waited for; matrix products, arithmetic and copies ran while one was open for 25% of the time, Pallas kernels for 0%

profile of v1, /device:TPU:4, one launch (start us, length us, event | category | flops | bytes accessed | tf_op | source)
XLA Modules:
  0.0 427.3 jit_solution(2582295379991983839)
XLA Ops:
  7.2 0.7 convert_element_type.100
  8.5 5.2 %all-to-all-start = ((bf16[128,16,1]{0,2,1:T(2,128)(2,1)}), bf16[128,16,1]{0,2,1:T(2,128)(2,1)S(1)}, u32[]{:S(2)}, u32[]{:S(2)}) async-start(bf16[128,16,1]{0,2,1:T(2,128)(2,1)} %broadcast_in_dim.28), calls=%async_computation | async-start | bytes 16384 | tf_op jit(solution)/shard_map/all_to_all | solution.py:99
  13.7 1.2 fusion.37
  15.0 3.1 fusion.40
  19.5 0.9 copy.77
  20.4 5.7 %all-to-all-start.5 = ((bf16[16,16,512]{2,0,1:T(8,128)(2,1)}), bf16[16,16,512]{2,0,1:T(8,128)(2,1)S(1)}, u32[]{:S(2)}, u32[]{:S(2)}) async-start(bf16[16,16,512]{2,0,1:T(8,128)(2,1)} %copy.77), calls=%async_computation.5 | async-start | bytes 524288 | tf_op jit(solution)/shard_map/all_to_all | solution.py:149
  26.3 7.8 %all-to-all-done.5 = bf16[16,16,512]{2,0,1:T(8,128)(2,1)S(1)} async-done(((bf16[16,16,512]{2,0,1:T(8,128)(2,1)}), bf16[16,16,512]{2,0,1:T(8,128)(2,1)S(1)}, u32[]{:S(2)}, u32[]{:S(2)}) %all-to-all-start.5) | async-done | bytes 262176 | tf_op jit(solution)/shard_map/all_to_all | solution.py:149
  34.1 0.9 broadcast_in_dim.29
  35.1 3.6 all-to-all-start.2
  38.7 6.8 %fusion.42 = f32[128,2048]{0,1:T(8,128)S(1)} fusion(bf16[2048,2048]{1,0:T(8,128)(2,1)} %param.17, bf16[128,2048]{1,0:T(8,128)(2,1)S(1)} %copy-done, f32[2048]{0:T(1024)S(1)} %copy-done.6, f32[128]{0:T(128)S(1)} %add_rsqrt_fusion.1), kind=kOutput, calls=%fused_computation.57 | convolution fusion | flops 1074790400 | bytes 9970176 | tf_op jit(solution)/shard_map/dot_general | solution.py:86
  46.3 0.9 pad_maximum_fusion
  47.1 2.3 all-to-all-done.2
  49.5 3.6 all-to-all-start.1
  54.3 0.9 copy.72
  55.4 8.5 %all-to-all-done.1 = bf16[128,16,128]{0,2,1:T(8,128)(2,1)S(1)} async-done(((bf16[128,16,128]{0,2,1:T(8,128)(2,1)}), bf16[128,16,128]{0,2,1:T(8,128)(2,1)S(1)}, u32[]{:S(2)}, u32[]{:S(2)}) %all-to-all-start.1) | async-done | bytes 524320 | tf_op jit(solution)/shard_map/all_to_all | solution.py:97
  64.5 71.2 %while.12 = (s32[]{:T(128)}, bf16[4,512,128]{2,1,0:T(8,128)(2,1)}, s32[4]{0:T(128)S(1)}, s32[2048]{0:T(1024)S(1)}, pred[2048]{0:T(1024)(128)(4,1)S(1)}, /*index=...) while((s32[]{:T(128)}, bf16[4,512,128]{2,1,0:T(8,128)(2,1)}, ...), condition=%wide.region_4.5_spmd.clone.clone, body=%wide.region_1.0_spmd.clone.clone.sunk | while | flops 555813376 | bytes 20214460 | solution.py:130
  65.8 3.6 fusion.77
  69.5 7.2 %fusion.78 = (f32[2,512]{1,0:T(2,128)S(1)}, f32[2,512,2048]{2,1,0:T(8,128)}) fusion(pred[512,2048]{1,0:T(8,128)(4,1)S(1)} %fusion.77, bf16[2048,64]{0,1:T(8,128)(2,1)} %get-tuple-element.220, bf16[2048,2,64]{0,2,1:T(8,128)(2,1)S(1)} %get-tuple-element.219, s32[]{:T(128)S(6)} %select_n.41), kind=kOutput, calls=%fused_computation.76.clone.1 | convolution fusion | flops 276826112 | bytes 9834500 | tf_op jit(solution)/shard_map/while/body/eval_jaxpr/sub | solution.py:125
  76.6 4.9 %fusion.79 = bf16[2,512,64]{1,2,0:T(8,128)(2,1)S(1)} fusion(f32[2,512,2048]{2,1,0:T(8,128)} %get-tuple-element.188, f32[2,512]{1,0:T(2,128)S(1)} %get-tuple-element.189, bf16[2048,64]{0,1:T(8,128)(2,1)S(1)} %get-tuple-element.221), kind=kOutput, calls=%fused_computation.17.clone.1 | convolution fusion | flops 272695296 | bytes 8785920 | tf_op jit(solution)/shard_map/while/body/eval_jaxpr/hts,sd->thd/dot_general | solution.py:127
  81.7 0.7 constant_dynamic-update-slice_fusion.2
  83.7 3.6 fusion.77
  87.3 7.2 %fusion.78 = (f32[2,512]{1,0:T(2,128)S(1)}, f32[2,512,2048]{2,1,0:T(8,128)}) fusion(pred[512,2048]{1,0:T(8,128)(4,1)S(1)} %fusion.77, bf16[2048,64]{0,1:T(8,128)(2,1)} %get-tuple-element.220, bf16[2048,2,64]{0,2,1:T(8,128)(2,1)S(1)} %get-tuple-element.219, s32[]{:T(128)S(6)} %select_n.41), kind=kOutput, calls=%fused_computation.76.clone.1 | convolution fusion | flops 276826112 | bytes 9834500 | tf_op jit(solution)/shard_map/while/body/eval_jaxpr/sub | solution.py:125
  94.5 4.9 %fusion.79 = bf16[2,512,64]{1,2,0:T(8,128)(2,1)S(1)} fusion(f32[2,512,2048]{2,1,0:T(8,128)} %get-tuple-element.188, f32[2,512]{1,0:T(2,128)S(1)} %get-tuple-element.189, bf16[2048,64]{0,1:T(8,128)(2,1)S(1)} %get-tuple-element.221), kind=kOutput, calls=%fused_computation.17.clone.1 | convolution fusion | flops 272695296 | bytes 8785920 | tf_op jit(solution)/shard_map/while/body/eval_jaxpr/hts,sd->thd/dot_general | solution.py:127
  99.5 0.7 constant_dynamic-update-slice_fusion.2
  101.5 3.6 fusion.77
  105.1 7.2 %fusion.78 = (f32[2,512]{1,0:T(2,128)S(1)}, f32[2,512,2048]{2,1,0:T(8,128)}) fusion(pred[512,2048]{1,0:T(8,128)(4,1)S(1)} %fusion.77, bf16[2048,64]{0,1:T(8,128)(2,1)} %get-tuple-element.220, bf16[2048,2,64]{0,2,1:T(8,128)(2,1)S(1)} %get-tuple-element.219, s32[]{:T(128)S(6)} %select_n.41), kind=kOutput, calls=%fused_computation.76.clone.1 | convolution fusion | flops 276826112 | bytes 9834500 | tf_op jit(solution)/shard_map/while/body/eval_jaxpr/sub | solution.py:125
  112.3 4.8 %fusion.79 = bf16[2,512,64]{1,2,0:T(8,128)(2,1)S(1)} fusion(f32[2,512,2048]{2,1,0:T(8,128)} %get-tuple-element.188, f32[2,512]{1,0:T(2,128)S(1)} %get-tuple-element.189, bf16[2048,64]{0,1:T(8,128)(2,1)S(1)} %get-tuple-element.221), kind=kOutput, calls=%fused_computation.17.clone.1 | convolution fusion | flops 272695296 | bytes 8785920 | tf_op jit(solution)/shard_map/while/body/eval_jaxpr/hts,sd->thd/dot_general | solution.py:127
  119.3 3.6 fusion.77
  122.9 7.2 %fusion.78 = (f32[2,512]{1,0:T(2,128)S(1)}, f32[2,512,2048]{2,1,0:T(8,128)}) fusion(pred[512,2048]{1,0:T(8,128)(4,1)S(1)} %fusion.77, bf16[2048,64]{0,1:T(8,128)(2,1)} %get-tuple-element.220, bf16[2048,2,64]{0,2,1:T(8,128)(2,1)S(1)} %get-tuple-element.219, s32[]{:T(128)S(6)} %select_n.41), kind=kOutput, calls=%fused_computation.76.clone.1 | convolution fusion | flops 276826112 | bytes 9834500 | tf_op jit(solution)/shard_map/while/body/eval_jaxpr/sub | solution.py:125
  130.1 4.8 %fusion.79 = bf16[2,512,64]{1,2,0:T(8,128)(2,1)S(1)} fusion(f32[2,512,2048]{2,1,0:T(8,128)} %get-tuple-element.188, f32[2,512]{1,0:T(2,128)S(1)} %get-tuple-element.189, bf16[2048,64]{0,1:T(8,128)(2,1)S(1)} %get-tuple-element.221), kind=kOutput, calls=%fused_computation.17.clone.1 | convolution fusion | flops 272695296 | bytes 8785920 | tf_op jit(solution)/shard_map/while/body/eval_jaxpr/hts,sd->thd/dot_general | solution.py:127
  135.7 3.6 all-to-all-start.3
  140.4 0.9 copy.79
  141.2 8.9 %all-to-all-done.3 = bf16[16,128,128]{2,1,0:T(8,128)(2,1)S(1)} async-done(((bf16[16,128,128]{2,1,0:T(8,128)(2,1)}), bf16[16,128,128]{2,1,0:T(8,128)(2,1)S(1)}, u32[]{:S(2)}, u32[]{:S(2)}) %all-to-all-start.3) | async-done | bytes 524320 | tf_op jit(solution)/shard_map/all_to_all | solution.py:132
  150.1 3.5 all-to-all-start.6
  154.0 4.7 %multiply_reduce_fusion = (f32[128]{0:T(128)S(1)}, f32[128,2048]{1,0:T(8,128)S(1)}) fusion(bf16[128,2048]{0,1:T(8,128)(2,1)S(1)} %bitcast.113, bf16[2048,2048]{1,0:T(8,128)(2,1)} %param.19, bf16[128,2048]{1,0:T(8,128)(2,1)S(1)} %copy-done), kind=kOutput, calls=%fused_computation.44 | convolution fusion | flops 1075314560 | bytes 10486272 | tf_op jit(solution)/shard_map/dot_general | solution.py:134
  158.9 2.8 all-to-all-done.6
  161.7 4.3 %stack.2 = bf16[16,128,2048]{2,1,0:T(8,128)(2,1)} broadcast(bf16[128,2048]{1,0:T(8,128)(2,1)S(1)} %multiply_convert_fusion.1), dimensions={1,2} | broadcast | bytes 8912896 | tf_op jit(solution)/shard_map/stack | solution.py:18
  166.0 4.9 %all-to-all-start.4 = ((bf16[16,128,2048]{2,1,0:T(8,128)(2,1)}), bf16[16,128,2048]{2,1,0:T(8,128)(2,1)}, u32[]{:S(2)}, u32[]{:S(2)}) async-start(bf16[16,128,2048]{2,1,0:T(8,128)(2,1)} %stack.2), calls=%async_computation.4 | async-start | bytes 16777216 | tf_op jit(solution)/shard_map/all_to_all | solution.py:17
  170.9 0.7 convert_element_type.113
  171.7 0.7 all-gather.6.cloned.1.call-update
  172.7 110.3 %all-to-all-done.4 = bf16[16,128,2048]{2,1,0:T(8,128)(2,1)} async-done(((bf16[16,128,2048]{2,1,0:T(8,128)(2,1)}), bf16[16,128,2048]{2,1,0:T(8,128)(2,1)}, u32[]{:S(2)}, u32[]{:S(2)}) %all-to-all-start.4) | async-done | bytes 8388640 | tf_op jit(solution)/shard_map/all_to_all | solution.py:17
  283.0 10.5 %fusion.57 = f32[2048,512]{1,0:T(8,128)} fusion(bf16[2048,2048]{1,0:T(8,128)(2,1)} %bitcast.21, bf16[2048,512]{1,0:T(8,128)(2,1)} %all-gather.4.cloned.1.call-done), kind=kOutput, calls=%fused_computation.77 | convolution fusion | flops 4294967296 | bytes 14680064 | tf_op jit(solution)/shard_map/dot_general | solution.py:158
  293.4 7.4 %all-gather.6.cloned.1.call-done = bf16[2048,512]{1,0:T(8,128)(2,1)} async-done(((bf16[256,512]{1,0:T(8,128)(2,1)}), bf16[2048,512]{1,0:T(8,128)(2,1)}) %all-gather.6.cloned.1.call-update) | async-done | bytes 2097168 | tf_op jit(solution)/shard_map/all_gather | solution.py:156
  300.9 15.2 %convolution_convert_fusion.1 = bf16[2048,2048]{1,0:T(8,128)(2,1)} fusion(bf16[512,2048]{1,0:T(8,128)(2,1)} %all-gather.8.cloned.1.call-done, f32[2048,512]{1,0:T(8,128)} %fusion.57, bf16[2048,2048]{1,0:T(8,128)(2,1)} %bitcast.21, bf16[2048,512]{1,0:T(8,128)(2,1)} %all-gather.6.cloned.1.call-done), kind=kOutput, calls=%fused_computation.32 | convolution fusion | flops 8600420352 | bytes 25165824 | tf_op jit(solution)/shard_map/dot_general | solution.py:163
  317.6 18.0 %all_to_all.101 = bf16[8,2,16,1024]{3,2,1,0:T(8,128)(2,1)S(1)} all-to-all(bf16[8,2,16,1024]{3,2,1,0:T(8,128)(2,1)S(1)} %bitcast.121), channel_id=1, replica_groups=mesh['dp'=8,'mp'=16] {'dp'}, dimensions={0} | all-to-all | bytes 1048576 | tf_op jit(solution)/shard_map/all_to_all | solution.py:186
  335.6 82.4 %reduce-scatter.2.cloned.1.call-done = bf16[128,2048]{1,0:T(8,128)(2,1)} async-done(((bf16[2048,2048]{1,0:T(8,128)(2,1)}), bf16[128,2048]{1,0:T(8,128)(2,1)}) %reduce-scatter.2.cloned.1.call-update) | async-done | bytes 524304 | tf_op jit(solution)/shard_map/reduce_scatter | solution.py:162
  418.0 1.9 add_convert_fusion
  420.0 0.8 copy.101
  (86 shorter events, 12.0 us)
Async XLA Ops:
  7.2 11.3 %copy-start.3 = (f32[16,8192]{1,0:T(8,128)S(1)}, f32[16,8192]{1,0:T(8,128)}, u32[]{:S(2)}) copy-start(f32[16,8192]{1,0:T(8,128)} %param.20) | copy-start | bytes 1572868
  8.5 11.9 %all-to-all-start = ((bf16[128,16,1]{0,2,1:T(2,128)(2,1)}), bf16[128,16,1]{0,2,1:T(2,128)(2,1)S(1)}, u32[]{:S(2)}, u32[]{:S(2)}) async-start(bf16[128,16,1]{0,2,1:T(2,128)(2,1)} %broadcast_in_dim.28), calls=%async_computation | async-start | bytes 16384 | tf_op jit(solution)/shard_map/all_to_all | solution.py:99
  18.3 20.3 %copy-start = (bf16[128,2048]{1,0:T(8,128)(2,1)S(1)}, bf16[128,2048]{1,0:T(8,128)(2,1)}, u32[]{:S(2)}) copy-start(bf16[128,2048]{1,0:T(8,128)(2,1)} %param.14) | copy-start | bytes 1572868
  18.3 20.3 %copy-start.6 = (f32[2048]{0:T(1024)S(1)}, f32[2048]{0:T(1024)}, u32[]{:S(2)}) copy-start(f32[2048]{0:T(1024)} %param.15) | copy-start | bytes 24580
  20.4 13.8 %all-to-all-start.5 = ((bf16[16,16,512]{2,0,1:T(8,128)(2,1)}), bf16[16,16,512]{2,0,1:T(8,128)(2,1)S(1)}, u32[]{:S(2)}, u32[]{:S(2)}) async-start(bf16[16,16,512]{2,0,1:T(8,128)(2,1)} %copy.77), calls=%async_computation.5 | async-start | bytes 524288 | tf_op jit(solution)/shard_map/all_to_all | solution.py:149
  34.1 11.3 %copy-start.1 = (bf16[16,16,512]{2,0,1:T(8,128)(2,1)}, bf16[16,16,512]{2,0,1:T(8,128)(2,1)S(1)}, u32[]{:S(2)}) copy-start(bf16[16,16,512]{2,0,1:T(8,128)(2,1)S(1)} %all-to-all-done.5) | copy-start | bytes 786436
  35.1 14.4 %all-to-all-start.2 = ((bf16[128,16,128]{0,2,1:T(8,128)(2,1)}), bf16[128,16,128]{0,2,1:T(8,128)(2,1)S(1)}, u32[]{:S(2)}, u32[]{:S(2)}) async-start(bf16[128,16,128]{0,2,1:T(8,128)(2,1)} %bitcast.10), calls=%async_computation.2 | async-start | bytes 1048576 | tf_op jit(solution)/shard_map/all_to_all | solution.py:98
  49.5 14.4 %all-to-all-start.1 = ((bf16[128,16,128]{0,2,1:T(8,128)(2,1)}), bf16[128,16,128]{0,2,1:T(8,128)(2,1)S(1)}, u32[]{:S(2)}, u32[]{:S(2)}) async-start(bf16[128,16,128]{0,2,1:T(8,128)(2,1)} %bitcast.5), calls=%async_computation.1 | async-start | bytes 1048576 | tf_op jit(solution)/shard_map/all_to_all | solution.py:97
  53.0 119.7 %all-gather.4.cloned.1.call-start = ((), (), s32[]{:S(2)}) async-start(), calls=%async_computation.9 | async-start | bytes 2359296 | tf_op jit(solution)/shard_map/all_gather | solution.py:155
  64.5 74.8 %copy-start.4 = (f32[16,8192]{1,0:T(8,128)S(1)}, f32[16,8192]{1,0:T(8,128)}, u32[]{:S(2)}) copy-start(f32[16,8192]{1,0:T(8,128)} %param.21) | copy-start | bytes 1572868
  135.7 14.4 %all-to-all-start.3 = ((bf16[16,128,128]{2,1,0:T(8,128)(2,1)}), bf16[16,128,128]{2,1,0:T(8,128)(2,1)S(1)}, u32[]{:S(2)}, u32[]{:S(2)}) async-start(bf16[16,128,128]{2,1,0:T(8,128)(2,1)} %bitcast.126), calls=%async_computation.3 | async-start | bytes 1048576 | tf_op jit(solution)/shard_map/all_to_all | solution.py:132
  150.1 11.6 %all-to-all-start.6 = ((bf16[16,16,512]{2,0,1:T(8,128)(2,1)}), bf16[16,16,512]{2,0,1:T(8,128)(2,1)S(1)}, u32[]{:S(2)}, u32[]{:S(2)}) async-start(bf16[16,16,512]{2,0,1:T(8,128)(2,1)} %copy.79), calls=%async_computation.6 | async-start | bytes 524288 | tf_op jit(solution)/shard_map/all_to_all | solution.py:150
  153.9 4.8 %copy-start.7 = (f32[2048]{0:T(1024)S(1)}, f32[2048]{0:T(1024)}, u32[]{:S(2)}) copy-start(f32[2048]{0:T(1024)} %param.16) | copy-start | bytes 24580
  161.7 4.3 %copy-start.2 = (bf16[16,16,512]{2,0,1:T(8,128)(2,1)}, bf16[16,16,512]{2,0,1:T(8,128)(2,1)S(1)}, u32[]{:S(2)}) copy-start(bf16[16,16,512]{2,0,1:T(8,128)(2,1)S(1)} %all-to-all-done.6) | copy-start | bytes 786436
  166.0 5.0 %copy-start.5 = (f32[64,2048]{1,0:T(8,128)S(1)}, f32[64,2048]{1,0:T(8,128)}, u32[]{:S(2)}) copy-start(f32[64,2048]{1,0:T(8,128)} %param.22) | copy-start | bytes 1572868
  166.0 117.0 %all-to-all-start.4 = ((bf16[16,128,2048]{2,1,0:T(8,128)(2,1)}), bf16[16,128,2048]{2,1,0:T(8,128)(2,1)}, u32[]{:S(2)}, u32[]{:S(2)}) async-start(bf16[16,128,2048]{2,1,0:T(8,128)(2,1)} %stack.2), calls=%async_computation.4 | async-start | bytes 16777216 | tf_op jit(solution)/shard_map/all_to_all | solution.py:17
  170.9 122.6 %all-gather.8.cloned.1.call-start = ((), (), s32[]{:S(2)}) async-start(), calls=%async_computation.11 | async-start | bytes 2359296 | tf_op jit(solution)/shard_map/all_gather | solution.py:161
  171.7 129.2 %all-gather.6.cloned.1.call-start = ((), (), s32[]{:S(2)}) async-start(), calls=%async_computation.10 | async-start | bytes 2359296 | tf_op jit(solution)/shard_map/all_gather | solution.py:156
  172.4 245.6 %reduce-scatter.2.cloned.1.call-start = ((), (), s32[]{:S(2)}) async-start(), calls=%async_computation.12 | async-start | bytes 8912896 | tf_op jit(solution)/shard_map/reduce_scatter | solution.py:162
  316.1 0.7 copy-start.8
Sparse Core Ops, SparseCore 0:
  56.2 54.2 all-gather.3
  174.6 68.3 all-gather.7
  246.0 54.8 all-gather.5
  316.3 101.7 reduce-scatter.1
